TPU v7x, 256 devices: a whole 4x4x8 slice. The times are simulated.
256 devices in a mesh: kv: 4 (over y), blk: 64 (over z, x, core).
Axes of the slice: x: 4, y: 4, z: 8, core: 2. Of those that a mesh axis runs over, the one named last changes fastest.
Arguments:
- embeds: bfloat16 [3, 512, 4096], P(None, None, 'blk'), may hold values from -6 to 6
- attn_gain: float32 [4096], P('blk'), may hold values from 0.25 to 1.75
- w_query: bfloat16 [4096, 4096], P('blk', 'kv'), may hold values from -0.1875 to 0.1875
- w_key: bfloat16 [4096, 512], P('blk', 'kv'), may hold values from -0.09375 to 0.09375
- w_value: bfloat16 [4096, 512], P('blk', 'kv'), may hold values from -0.09375 to 0.09375
- w_out: bfloat16 [4096, 4096], P('kv', 'blk'), may hold values from -0.375 to 0.375
- cache_kv: bfloat16 [2048, 4, 2, 128, 128], P('blk', 'kv'), may hold values from -102 to 102, as said below
- lengths: int32 [512], replicated, may hold values from 1 to 8192, as said below
- block_table: int32 [512, 64], replicated, may hold values from 0 to 2048, as said below
- parents: int32 [3, 512], replicated, may hold values from 0 to 511, as said below
Outputs:
- out_rows: bfloat16 [3, 512, 4096], P(None, None, 'blk')
- appended: bfloat16 [3, 512, 4, 2, 128], P(None, 'blk', 'kv')
Inputs may be any that keep to these rules, and one draw needn't show every extreme that they name: `lengths`: one beam holds exactly 8192 tokens. `block_table`: row b names the slots of beam b's blocks of 128 tokens in order; entries at and past ceil(lengths[b] / 128) equal 2048; no slot is named twice. parents[s, b] lies in the aligned group of 8 beams that holds b. `cache_kv`: slots that no row of block_table names are never read.
All inputs are finite; a program needn't handle non-finite values.
Results may differ from a plain program's by a relative error of at most 0.0044.
The roundings to bfloat16 on the way count: a program that leaves them out, or rounds other values in their place, can miss the bound.
Values may be sent and summed in bfloat16 or wider, within the bound.
No kernel may reach another device: no remote copies, remote signals or barrier semaphores. Data moves between devices by JAX's collectives and lax.ppermute only.
A program may use at most 64 MiB of HBM per device.

v0:
```python
import math
import jax
import jax.numpy as jnp
from jax import lax
from jax.sharding import PartitionSpec as P

GROUP = 8
NEGATIVE = -1e30
EPSILON = 1e-05
ROPE_BASE = 5000000.0


def rotate(vector, position):
    half_dim = vector.shape[-1] // 2
    exponent = jnp.arange(half_dim, dtype=jnp.float32) * (2.0 / vector.shape[-1])
    frequency = ROPE_BASE ** (-exponent)
    angles = position.astype(jnp.float32)[:, None] * frequency[None, :]
    target_shape = (position.shape[0],) + (1,) * (vector.ndim - 2) + (half_dim,)
    cosines = jnp.cos(angles).reshape(target_shape)
    sine_part = jnp.sin(angles).reshape(target_shape)
    first_half = vector[..., :half_dim]
    second_half = vector[..., half_dim:]
    return jnp.concatenate(
        [
            first_half * cosines - second_half * sine_part,
            second_half * cosines + first_half * sine_part,
        ],
        axis=-1,
    )


def body(
    embeds, attn_gain, w_query, w_key, w_value, w_out, cache_kv, lengths, block_table, parents
):
    axis_count = lax.axis_size("blk")
    shard_index = lax.axis_index("blk")
    step_total, beam_count, width_part = embeds.shape
    beams_here = beam_count // axis_count
    slot_count = cache_kv.shape[0]
    total_slots = slot_count * axis_count
    block_len = cache_kv.shape[3]
    head_dim = cache_kv.shape[4]
    heads_per_group = w_query.shape[1] // head_dim
    group_count = beam_count // GROUP
    model_width = width_part * axis_count
    scaling = 1.0 / math.sqrt(head_dim)
    row_offset = shard_index * beams_here
    joined_weights = jnp.concatenate([w_query, w_key, w_value], axis=1)
    cached_keys = cache_kv[:, 0, 0]
    cached_values = cache_kv[:, 0, 1]
    max_blocks = block_table.shape[1]
    beam_ids = jnp.broadcast_to(jnp.arange(beam_count, dtype=jnp.int32)[:, None], block_table.shape)
    block_ids = jnp.broadcast_to(
        jnp.arange(max_blocks, dtype=jnp.int32)[None, :], block_table.shape
    )
    flat_table = block_table.reshape(-1)
    owner_all = jnp.full((total_slots + 1,), -1, jnp.int32).at[flat_table].set(beam_ids.reshape(-1))
    logical_all = jnp.zeros((total_slots + 1,), jnp.int32).at[flat_table].set(block_ids.reshape(-1))
    owner_beam = lax.dynamic_slice_in_dim(owner_all, shard_index * slot_count, slot_count)
    logical_block = lax.dynamic_slice_in_dim(logical_all, shard_index * slot_count, slot_count)
    filled = owner_beam >= 0
    safe_owner = jnp.maximum(owner_beam, 0)
    group_of = safe_owner // GROUP
    group_onehot = (
        (group_of[:, None] == jnp.arange(group_count, dtype=jnp.int32)[None, :]) & filled[:, None]
    ).astype(jnp.float32)
    token_index = jnp.arange(block_len, dtype=jnp.int32)
    in_length = (
        logical_block[:, None] * block_len + token_index[None, :] < lengths[safe_owner][:, None]
    )
    members = group_of[:, None] * GROUP + jnp.arange(GROUP, dtype=jnp.int32)[None, :]
    root_beams = jnp.arange(beam_count, dtype=jnp.int32)
    new_keys = jnp.zeros((step_total, beams_here, head_dim), jnp.bfloat16)
    new_values = jnp.zeros((step_total, beams_here, head_dim), jnp.bfloat16)
    outputs = []
    for step_index in range(step_total):
        root_beams = root_beams[parents[step_index]]
        local_parent = (
            lax.dynamic_slice_in_dim(parents[step_index], row_offset, beams_here) - row_offset
        )
        new_keys = new_keys[:, local_parent]
        new_values = new_values[:, local_parent]
        stream = embeds[step_index].astype(jnp.float32)
        squares = lax.psum(jnp.sum(stream * stream, axis=1), "blk")
        inverse_rms = lax.rsqrt(squares / model_width + EPSILON)
        normed = (stream * inverse_rms[:, None] * attn_gain[None, :]).astype(jnp.bfloat16)
        projected = lax.psum_scatter(
            jnp.dot(normed, joined_weights, preferred_element_type=jnp.float32),
            "blk",
            scatter_dimension=0,
            tiled=True,
        )
        position = (
            lax.dynamic_slice_in_dim(lengths[root_beams], row_offset, beams_here) + step_index
        )
        rotated_query = rotate(
            projected[:, : heads_per_group * head_dim].reshape(
                beams_here, heads_per_group, head_dim
            ),
            position,
        ).astype(jnp.bfloat16)
        key_new = rotate(
            projected[:, heads_per_group * head_dim : (heads_per_group + 1) * head_dim], position
        ).astype(jnp.bfloat16)
        value_new = projected[:, (heads_per_group + 1) * head_dim :].astype(jnp.bfloat16)
        new_keys = new_keys.at[step_index].set(key_new)
        new_values = new_values.at[step_index].set(value_new)
        queries = lax.all_gather(
            rotated_query.reshape(beams_here, heads_per_group * head_dim), "blk", axis=0, tiled=True
        )
        slot_query = queries.reshape(group_count, GROUP * heads_per_group, head_dim)[group_of]
        scores = (
            jnp.einsum("sqd,skd->sqk", slot_query, cached_keys, preferred_element_type=jnp.float32)
            * scaling
        )
        scores = scores.reshape(slot_count, GROUP, heads_per_group, block_len)
        active = ((root_beams[members] == owner_beam[:, None])[:, :, None] & in_length[:, None, :])[
            :, :, None, :
        ]
        slot_top = jnp.max(jnp.where(active, scores, NEGATIVE), axis=-1)
        group_top = jnp.max(
            jnp.where(group_onehot[:, :, None, None] > 0, slot_top[:, None], NEGATIVE), axis=0
        ).reshape(beam_count, heads_per_group)
        latest_key_rows = new_keys[: step_index + 1]
        new_scores = (
            jnp.einsum(
                "pam,fpm->paf", rotated_query, latest_key_rows, preferred_element_type=jnp.float32
            )
            * scaling
        )
        own_top = jnp.maximum(
            lax.dynamic_slice_in_dim(group_top, row_offset, beams_here),
            jnp.max(new_scores, axis=-1),
        )
        local_top = lax.dynamic_update_slice_in_dim(group_top, own_top, row_offset, 0)
        ceiling = lax.pmax(local_top, "blk")
        slot_ceiling = ceiling.reshape(group_count, GROUP, heads_per_group)[group_of]
        prob_weights = jnp.exp(jnp.where(active, scores - slot_ceiling[..., None], NEGATIVE))
        slot_denominator = jnp.sum(prob_weights, axis=-1)
        slot_numer = jnp.einsum(
            "sgqk,skd->sgqd",
            prob_weights.astype(jnp.bfloat16),
            cached_values,
            preferred_element_type=jnp.float32,
        )
        numerator = jnp.einsum(
            "sg,sx->gx",
            group_onehot,
            slot_numer.reshape(slot_count, -1),
            precision=lax.Precision.HIGHEST,
        ).reshape(beam_count, heads_per_group, head_dim)
        denominator = jnp.einsum(
            "sg,sx->gx",
            group_onehot,
            slot_denominator.reshape(slot_count, -1),
            precision=lax.Precision.HIGHEST,
        ).reshape(beam_count, heads_per_group)
        own_ceiling = lax.dynamic_slice_in_dim(ceiling, row_offset, beams_here)
        new_weights = jnp.exp(new_scores - own_ceiling[..., None])
        updated_denominator = jnp.sum(new_weights, axis=-1)
        new_numer = jnp.einsum(
            "pjz,zpc->pjc",
            new_weights.astype(jnp.bfloat16),
            new_values[: step_index + 1],
            preferred_element_type=jnp.float32,
        )
        numerator, denominator = (
            lax.psum_scatter(numerator, "blk", scatter_dimension=0, tiled=True),
            lax.psum_scatter(denominator, "blk", scatter_dimension=0, tiled=True),
        )
        own_rows = (
            ((numerator + new_numer) / (denominator + updated_denominator)[..., None])
            .astype(jnp.bfloat16)
            .reshape(beams_here, heads_per_group * head_dim)
        )
        attended = lax.all_gather(own_rows, "blk", axis=0, tiled=True)
        partial_value = jnp.dot(attended, w_out, preferred_element_type=jnp.float32)
        head_total = lax.psum(partial_value, "kv")
        outputs.append((stream + head_total).astype(jnp.bfloat16))
    appended = jnp.stack([new_keys, new_values], axis=2)[:, :, None]
    return (jnp.stack(outputs), appended)


def solution(mesh):
    return jax.shard_map(
        body,
        mesh=mesh,
        in_specs=(
            P(None, None, "blk"),
            P("blk"),
            P("blk", "kv"),
            P("blk", "kv"),
            P("blk", "kv"),
            P("kv", "blk"),
            P("blk", "kv", None, None, None),
            P(),
            P(),
            P(),
        ),
        out_specs=(P(None, None, "blk"), P(None, "blk", "kv", None, None)),
        check_vma=False,
    )
```

profile of v0, /device:TPU:2, one launch (start us, length us, event | category | flops | bytes accessed | tf_op | source)
XLA Modules:
  0.0 1692.4 jit_solution(13006681837210420839)
XLA Ops:
  9.2 128.5 %all-reduce.7 = (f32[512]{0:T(512)S(1)}, f32[512]{0:T(512)S(1)}, f32[512]{0:T(512)S(1)}) all-reduce(f32[512]{0:T(512)S(1)} %get-tuple-element.102, f32[512]{0:T(512)S(1)} %get-tuple-element.101, f32[512]{0:T(512)S(1)} %get-tuple-element.100), channel_id=1, replica_groups=mesh['kv'=4,'blk'=64] {'blk'}, use_global_device_ids=true, to_apply=%region_25.26 | all-reduce | flops 1536 | bytes 12288 | tf_op jit(solution)/shard_map/psum | solution.py:84
  139.2 3.0 fusion.73
  147.2 3.5 gather_fusion
  150.7 3.5 gather_fusion.6
  154.4 3.5 gather_fusion.3
  157.9 3.5 gather_fusion.14
  161.4 3.5 gather_fusion.16
  164.9 3.5 gather_fusion.8
  170.3 179.9 %all-reduce.14.cloned.1.call-done = (f32[512,1280]{1,0:T(8,128)}, f32[512,1280]{1,0:T(8,128)}, f32[512,1280]{1,0:T(8,128)}) async-done(((f32[512,1280]{1,0:T(8,128)}, f32[512,1280]{1,0:T(8,128)}, f32[512,1280]{1,0:T(8,128)}), (f32[512,1280]{1,0:T(8,128)}, f32[512,1280]{1,0:T(8,128)}, f32[512,1280]{1,0:T(8,128)})) %all-reduce.14.cloned.1.call-update) | async-done | bytes 7864336
  353.0 120.1 %scatter_custom_fusion = s32[2049]{0:T(1024)S(1)} fusion(s32[32768]{0:T(1024)S(1)} %bitcast.296, s32[32768]{0:T(1024)S(1)} %reshape.1134, s32[]{:T(128)} %constant.196.clone.1), kind=kCustom, calls=%fused_computation.206 | custom fusion | bytes 8200 | tf_op jit(solution)/shard_map/scatter | solution.py:57
  482.0 120.1 %scatter_custom_fusion.1 = s32[2049]{0:T(1024)S(1)} fusion(s32[32768]{0:T(1024)S(1)} %bitcast.297, s32[32768]{0:T(1024)S(1)} %reshape.1142, s32[]{:T(128)} %constant.197.clone.1), kind=kCustom, calls=%fused_computation.204 | custom fusion | bytes 8200 | tf_op jit(solution)/shard_map/scatter | solution.py:58
  624.4 2.8 fusion.6
  629.4 49.9 %all-gather.15.cloned.1.call-done = bf16[512,1024]{1,0:T(8,128)(2,1)} async-done(((bf16[8,1024]{1,0:T(8,128)(2,1)}), bf16[512,1024]{1,0:T(8,128)(2,1)}) %all-gather.15.cloned.1.call-update) | async-done | bytes 1048592 | tf_op jit(solution)/shard_map/all_gather | solution.py:108
  681.6 2.8 gather_fusion.17
  684.4 2.9 fusion.12
  715.8 244.4 %all-reduce.9 = (f32[512,8]{0,1:T(8,128)}, f32[512,8]{0,1:T(8,128)}, f32[512,8]{0,1:T(8,128)}) all-reduce(f32[512,8]{0,1:T(8,128)} %dynamic_update_slice.11, f32[512,8]{0,1:T(8,128)S(1)} %dynamic_update_slice.10, f32[512,8]{0,1:T(8,128)} %copy-done.7), channel_id=1, replica_groups=mesh['kv'=4,'blk'=64] {'blk'}, use_global_device_ids=true, to_apply=%region_30.31 | all-reduce | flops 12288 | bytes 98304 | tf_op jit(solution)/shard_map/pmax | solution.py:136
  966.0 3.1 fusion.21
  977.2 3.1 fusion.18
  1006.3 252.8 %all-reduce.6 = (f32[512,8]{1,0:T(8,128)S(1)}, f32[512,8]{1,0:T(8,128)S(1)}, f32[512,8]{1,0:T(8,128)S(1)}) all-reduce(f32[512,8]{1,0:T(8,128)S(1)} %reshape.957, f32[512,8]{1,0:T(8,128)S(1)} %reshape.947, f32[512,8]{1,0:T(8,128)S(1)} %reshape.937), channel_id=10, replica_groups=mesh['kv'=4,'blk'=64] {'blk'}, use_global_device_ids=true, to_apply=%region_33.34.clone | all-reduce | flops 12288 | bytes 98304
  1268.0 133.9 %reduce-scatter.8.cloned.1.call-done = f32[8,8,128]{2,1,0:T(8,128)} async-done(((f32[512,8,128]{2,1,0:T(8,128)}), f32[8,8,128]{2,1,0:T(8,128)}) %reduce-scatter.8.cloned.1.call-update) | async-done | bytes 32784 | tf_op jit(solution)/shard_map/reduce_scatter | solution.py:168
  1403.6 76.2 %all-gather.9.cloned.1.call-done = bf16[512,1024]{1,0:T(8,128)(2,1)} async-done(((bf16[8,1024]{1,0:T(8,128)(2,1)}), bf16[512,1024]{1,0:T(8,128)(2,1)}) %all-gather.9.cloned.1.call-update) | async-done | bytes 1048592 | tf_op jit(solution)/shard_map/all_gather | solution.py:176
  1482.1 74.9 %all-gather.13.cloned.1.call-done = bf16[512,1024]{1,0:T(8,128)(2,1)} async-done(((bf16[8,1024]{1,0:T(8,128)(2,1)}), bf16[512,1024]{1,0:T(8,128)(2,1)}) %all-gather.13.cloned.1.call-update) | async-done | bytes 1048592 | tf_op jit(solution)/shard_map/all_gather | solution.py:176
  1559.3 75.3 %all-gather.17.cloned.1.call-done = bf16[512,1024]{1,0:T(8,128)(2,1)} async-done(((bf16[8,1024]{1,0:T(8,128)(2,1)}), bf16[512,1024]{1,0:T(8,128)(2,1)}) %all-gather.17.cloned.1.call-update) | async-done | bytes 1048592 | tf_op jit(solution)/shard_map/all_gather | solution.py:176
  1637.7 46.4 %all-reduce.16.cloned.1.call-done = (f32[512,64]{0,1:T(8,128)}, f32[512,64]{0,1:T(8,128)}, f32[512,64]{0,1:T(8,128)}) async-done(((f32[512,64]{0,1:T(8,128)}, f32[512,64]{0,1:T(8,128)}, f32[512,64]{0,1:T(8,128)}), (f32[512,64]{0,1:T(8,128)}, f32[512,64]{0,1:T(8,128)}, f32[512,64]{0,1:T(8,128)})) %all-reduce.16.cloned.1.call-update) | async-done | bytes 393232 | tf_op jit(solution)/shard_map/psum | solution.py:178
  (279 shorter events, 135.9 us)
Async XLA Ops:
  7.2 1472.6 %copy-start = (bf16[1024,64]{0,1:T(8,128)(2,1)S(1)}, bf16[1024,64]{0,1:T(8,128)(2,1)}, u32[]{:S(2)}) copy-start(bf16[1024,64]{0,1:T(8,128)(2,1)} %param.27) | copy-start | bytes 393220
  7.2 135.0 %copy-start.5 = (bf16[3,512,64]{1,2,0:T(8,128)(2,1)S(1)}, bf16[3,512,64]{1,2,0:T(8,128)(2,1)}, u32[]{:S(2)}) copy-start(bf16[3,512,64]{1,2,0:T(8,128)(2,1)} %param.22) | copy-start | bytes 589828
  7.2 135.0 %copy-start.32 = (f32[64]{0:T(128)S(1)}, f32[64]{0:T(128)}, u32[]{:S(2)}) copy-start(f32[64]{0:T(128)} %param.23) | copy-start | bytes 772
  7.2 343.0 %all-reduce.14.cloned.1.call-start = ((), (), s32[]{:S(2)}) async-start(), calls=%async_computation.12 | async-start | bytes 15728640
  146.5 465.7 %all-gather.11.cloned.1.call-start = ((), (), s32[]{:S(2)}) async-start(), calls=%async_computation.6 | async-start | bytes 1064960 | tf_op jit(solution)/shard_map/all_gather | solution.py:108
  154.3 454.4 %copy-start.30 = (s32[1024]{0:T(1024)}, s32[1024]{0:T(1024)S(1)}, u32[]{:S(2)}) copy-start(s32[1024]{0:T(1024)S(1)} %get-tuple-element.185) | copy-start | bytes 12292
  352.7 266.6 %all-gather.7.cloned.1.call-start = ((), (), s32[]{:S(2)}) async-start(), calls=%async_computation.3 | async-start | bytes 1064960 | tf_op jit(solution)/shard_map/all_gather | solution.py:108
  473.2 129.1 %copy-start.17 = (pred[32]{0:T(512)(128)(4,1)}, pred[32]{0:T(512)(128)(4,1)S(1)}, u32[]{:S(2)}) copy-start(pred[32]{0:T(512)(128)(4,1)S(1)} %get-tuple-element.121) | copy-start | bytes 100
  474.8 204.5 %all-gather.15.cloned.1.call-start = ((), (), s32[]{:S(2)}) async-start(), calls=%async_computation.9 | async-start | bytes 1064960 | tf_op jit(solution)/shard_map/all_gather | solution.py:108
  482.0 133.2 %copy-start.2 = (bf16[32,1,2,128,128]{4,3,2,1,0:T(8,128)(2,1)S(1)}, bf16[32,1,2,128,128]{4,3,2,1,0:T(8,128)(2,1)}, u32[]{:S(2)}) copy-start(bf16[32,1,2,128,128]{4,3,2,1,0:T(8,128)(2,1)} %param.28) | copy-start | bytes 6291460
  604.8 655.3 %reduce-scatter.4.cloned.1.call-start = ((), (), s32[]{:S(2)}) async-start(), calls=%async_computation.4 | async-start | bytes 2129920 | tf_op jit(solution)/shard_map/reduce_scatter | solution.py:168
  971.8 292.3 %reduce-scatter.6.cloned.1.call-start = ((), (), s32[]{:S(2)}) async-start(), calls=%async_computation.7 | async-start | bytes 2129920 | tf_op jit(solution)/shard_map/reduce_scatter | solution.py:168
  983.0 419.0 %reduce-scatter.8.cloned.1.call-start = ((), (), s32[]{:S(2)}) async-start(), calls=%async_computation.10 | async-start | bytes 2129920 | tf_op jit(solution)/shard_map/reduce_scatter | solution.py:168
  991.9 487.9 %all-gather.9.cloned.1.call-start = ((), (), s32[]{:S(2)}) async-start(), calls=%async_computation.5 | async-start | bytes 1064960 | tf_op jit(solution)/shard_map/all_gather | solution.py:176
  1001.5 257.6 %copy-start.11 = (f32[8,1,8]{0,2,1:T(8,128)S(1)}, f32[8,1,8]{0,2,1:T(8,128)}, u32[]{:S(2)}) copy-start(f32[8,1,8]{0,2,1:T(8,128)} %copy.332) | copy-start | bytes 772
  1001.6 258.5 %copy-start.16 = (f32[8,128]{1,0:T(8,128)S(1)}, f32[8,128]{1,0:T(8,128)}, u32[]{:S(2)}) copy-start(f32[8,128]{1,0:T(8,128)} %get-tuple-element.131) | copy-start | bytes 12292
  1001.7 259.9 %copy-start.29 = (bf16[1,8,128]{2,1,0:T(8,128)(2,1)S(1)}, bf16[1,8,128]{2,1,0:T(8,128)(2,1)}, u32[]{:S(2)}) copy-start(bf16[1,8,128]{2,1,0:T(8,128)(2,1)} %get-tuple-element.132) | copy-start | bytes 6148
  1001.7 259.9 %copy-start.14 = (bf16[3,8,128]{2,0,1:T(4,128)(2,1)S(1)}, bf16[3,8,128]{2,0,1:T(4,128)(2,1)}, u32[]{:S(2)}) copy-start(bf16[3,8,128]{2,0,1:T(4,128)(2,1)} %copy.390) | copy-start | bytes 18436
  1001.7 262.3 %copy-start.28 = (f32[8,8,2]{1,2,0:T(2,128)S(1)}, f32[8,8,2]{1,2,0:T(2,128)}, u32[]{:S(2)}) copy-start(f32[8,8,2]{1,2,0:T(2,128)} %get-tuple-element.180) | copy-start | bytes 1540
  1002.6 265.4 %copy-start.8 = (f32[8,8,3]{1,2,0:T(4,128)S(1)}, f32[8,8,3]{1,2,0:T(4,128)}, u32[]{:S(2)}) copy-start(f32[8,8,3]{1,2,0:T(4,128)} %get-tuple-element.178) | copy-start | bytes 2308
  1261.5 295.5 %all-gather.13.cloned.1.call-start = ((), (), s32[]{:S(2)}) async-start(), calls=%async_computation.8 | async-start | bytes 1064960 | tf_op jit(solution)/shard_map/all_gather | solution.py:176
  1265.7 369.0 %all-gather.17.cloned.1.call-start = ((), (), s32[]{:S(2)}) async-start(), calls=%async_computation.11 | async-start | bytes 1064960 | tf_op jit(solution)/shard_map/all_gather | solution.py:176
  1403.5 233.5 %copy-start.10 = (bf16[3,8,128]{2,0,1:T(4,128)(2,1)S(1)}, bf16[3,8,128]{2,0,1:T(4,128)(2,1)}, u32[]{:S(2)}) copy-start(bf16[3,8,128]{2,0,1:T(4,128)(2,1)} %copy-done.9) | copy-start | bytes 18436
  1403.6 280.5 %all-reduce.16.cloned.1.call-start = ((), (), s32[]{:S(2)}) async-start(), calls=%async_computation.13 | async-start | bytes 786432 | tf_op jit(solution)/shard_map/psum | solution.py:178
  (21 other events, 234.6 us)
Sparse Core Ops, SparseCore 0:
  146.6 203.5 all-reduce.13
  353.5 74.3 all-gather.10
  474.9 74.3 all-gather.6
  604.9 74.3 all-gather.14
  971.9 143.4 reduce-scatter.3
  1119.9 138.9 reduce-scatter.5
  1262.9 138.9 reduce-scatter.7
  1405.1 74.6 all-gather.8
  1482.9 74.0 all-gather.12
  1560.6 74.0 all-gather.16
  1637.9 46.1 all-reduce.15
where the time goes:
time: 1700 us; the launch traced here: 1690 us
  waiting for transfers between devices  637 us (37%)
  blocking collectives  626 us (37%)
  local copies, waits for them, and re-layouts  352 us (21%)
  matrix products  41.8 us (2%)
  other arithmetic  20.1 us (1%)
    unnamed x1, blocking collectives  253 us
    pmax x1, blocking collectives, body(): ceiling = lax.pmax(local_top, 'blk')  244 us
    all_gather x3, waiting for transfers between devices, body(): attended = lax.all_gather(own_rows, 'blk', axis=0, tiled=True)  226 us
    unnamed x12, waiting for transfers between devices  180 us
    reduce_scatter x3, waiting for transfers between devices, body(): lax.psum_scatter(numerator, 'blk', scatter_dimension=0, tiled=True)  134 us
    psum x1, blocking collectives, body(): squares = lax.psum(jnp.sum(stream * stream, axis=1), 'blk')  128 us
    scatter x1, local copies, waits for them, and re-layouts, body(): jnp.zeros((total_slots + 1,), jnp.int32).at[flat_table]  120 us
    scatter x1, local copies, waits for them, and re-layouts, body(): jnp.full((total_slots + 1,), -1, jnp.int32).at[flat_table]  120 us
  transfers between devices with their start and end apart: 11, of which 7 were waited for; matrix products, arithmetic and copies ran while one was open for 20% of the time, Pallas kernels for 0%

commit v1 on v0

--- a/solution.py
+++ b/solution.py
@@ -173,7 +173,9 @@
             .astype(jnp.bfloat16)
             .reshape(beams_here, heads_per_group * head_dim)
         )
-        attended = lax.all_gather(own_rows, "blk", axis=0, tiled=True)
+        attended = jnp.concatenate(
+            lax.all_to_all(jnp.stack([own_rows] * lax.axis_size("blk")), "blk", 0, 0), axis=0
+        )
         partial_value = jnp.dot(attended, w_out, preferred_element_type=jnp.float32)
         head_total = lax.psum(partial_value, "kv")
         outputs.append((stream + head_total).astype(jnp.bfloat16))

time: 1700 us -> 1520 us (0.89)
  waiting for transfers between devices: 637 us -> 429 us
  starting transfers between devices: 0.68 us -> 28 us
    all_gather x3 -> x0, waiting for transfers between devices: 226 us -> none  [body(): attended = lax.all_gather(own_rows, 'blk', axis=0, tiled=True)]
    all_to_all x0 -> x3, waiting for transfers between devices: none -> 44.4 us  [body(): lax.all_to_all(jnp.stack([own_rows] * lax.axis_size('blk')), 'blk', 0, 0)]
    all_to_all x0 -> x3, starting transfers between devices: none -> 27.5 us  [body(): lax.all_to_all(jnp.stack([own_rows] * lax.axis_size('blk')), 'blk', 0, 0)]
    reduce_scatter x3, waiting for transfers between devices: 134 us -> 107 us  [body(): lax.psum_scatter(numerator, 'blk', scatter_dimension=0, tiled=True)]
    unnamed x12 -> x9, waiting for transfers between devices: 180 us -> 180 us
  transfers between devices with their start and end apart: 11 -> 11, of which waited for: 7 -> 6; matrix products, arithmetic and copies ran while one was open for 20% -> 23% of each run, Pallas kernels for 0% -> 0%
where the time goes in v1:
time: 1520 us; the launch traced here: 1510 us
  blocking collectives  626 us (41%)
  waiting for transfers between devices  429 us (28%)
  local copies, waits for them, and re-layouts  349 us (23%)
  matrix products  40.5 us (3%)
  starting transfers between devices  28 us (2%)
  other arithmetic  23 us (2%)
  between operations  15.6 us (1%)
    unnamed x1, blocking collectives  254 us
    pmax x1, blocking collectives, body(): ceiling = lax.pmax(local_top, 'blk')  244 us
    unnamed x9, waiting for transfers between devices  180 us
    psum x1, blocking collectives, body(): squares = lax.psum(jnp.sum(stream * stream, axis=1), 'blk')  128 us
    scatter x1, local copies, waits for them, and re-layouts, body(): jnp.full((total_slots + 1,), -1, jnp.int32).at[flat_table]  120 us
    scatter x1, local copies, waits for them, and re-layouts, body(): jnp.zeros((total_slots + 1,), jnp.int32).at[flat_table]  120 us
    reduce_scatter x3, waiting for transfers between devices, body(): lax.psum_scatter(numerator, 'blk', scatter_dimension=0, tiled=True)  107 us
    all_gather x3, waiting for transfers between devices, body(): lax.all_gather(rotated_query.reshape(beams_here, heads_per_group * head_d...  53.8 us
  transfers between devices with their start and end apart: 11, of which 6 were waited for; matrix products, arithmetic and copies ran while one was open for 23% of the time, Pallas kernels for 0%

profile of v1, /device:TPU:2, one launch (start us, length us, event | category | flops | bytes accessed | tf_op | source)
XLA Modules:
  0.0 1512.0 jit_solution(1880767185828595789)
XLA Ops:
  9.2 128.5 %all-reduce.7 = (f32[512]{0:T(512)S(1)}, f32[512]{0:T(512)S(1)}, f32[512]{0:T(512)S(1)}) all-reduce(f32[512]{0:T(512)S(1)} %get-tuple-element.102, f32[512]{0:T(512)S(1)} %get-tuple-element.101, f32[512]{0:T(512)S(1)} %get-tuple-element.100), channel_id=1, replica_groups=mesh['kv'=4,'blk'=64] {'blk'}, use_global_device_ids=true, to_apply=%region_25.26 | all-reduce | flops 1536 | bytes 12288 | tf_op jit(solution)/shard_map/psum | solution.py:84
  139.2 3.0 fusion.79
  147.1 3.5 gather_fusion
  150.6 3.5 gather_fusion.6
  154.3 3.5 gather_fusion.3
  157.8 3.5 gather_fusion.14
  161.3 3.5 gather_fusion.16
  164.9 3.5 gather_fusion.8
  170.2 180.0 %all-reduce.14.cloned.1.call-done = (f32[512,1280]{1,0:T(8,128)}, f32[512,1280]{1,0:T(8,128)}, f32[512,1280]{1,0:T(8,128)}) async-done(((f32[512,1280]{1,0:T(8,128)}, f32[512,1280]{1,0:T(8,128)}, f32[512,1280]{1,0:T(8,128)}), (f32[512,1280]{1,0:T(8,128)}, f32[512,1280]{1,0:T(8,128)}, f32[512,1280]{1,0:T(8,128)})) %all-reduce.14.cloned.1.call-update) | async-done | bytes 7864336
  353.0 120.1 %scatter_custom_fusion = s32[2049]{0:T(1024)S(1)} fusion(s32[32768]{0:T(1024)S(1)} %bitcast.302, s32[32768]{0:T(1024)S(1)} %reshape.1140, s32[]{:T(128)} %constant.196.clone.1), kind=kCustom, calls=%fused_computation.212 | custom fusion | bytes 8200 | tf_op jit(solution)/shard_map/scatter | solution.py:57
  482.0 120.1 %scatter_custom_fusion.1 = s32[2049]{0:T(1024)S(1)} fusion(s32[32768]{0:T(1024)S(1)} %bitcast.303, s32[32768]{0:T(1024)S(1)} %reshape.1148, s32[]{:T(128)} %constant.197.clone.1), kind=kCustom, calls=%fused_computation.210 | custom fusion | bytes 8200 | tf_op jit(solution)/shard_map/scatter | solution.py:58
  621.8 2.9 fusion.6
  625.5 53.7 %all-gather.8.cloned.1.call-done = bf16[512,1024]{1,0:T(8,128)(2,1)} async-done(((bf16[8,1024]{1,0:T(8,128)(2,1)}), bf16[512,1024]{1,0:T(8,128)(2,1)}) %all-gather.8.cloned.1.call-update) | async-done | bytes 1048592 | tf_op jit(solution)/shard_map/all_gather | solution.py:108
  712.7 244.4 %all-reduce.9 = (f32[512,8]{0,1:T(8,128)}, f32[512,8]{0,1:T(8,128)}, f32[512,8]{0,1:T(8,128)}) all-reduce(f32[512,8]{0,1:T(8,128)} %dynamic_update_slice.11, f32[512,8]{0,1:T(8,128)S(1)} %dynamic_update_slice.10, f32[512,8]{0,1:T(8,128)} %copy-done.5), channel_id=1, replica_groups=mesh['kv'=4,'blk'=64] {'blk'}, use_global_device_ids=true, to_apply=%region_30.31 | all-reduce | flops 12288 | bytes 98304 | tf_op jit(solution)/shard_map/pmax | solution.py:136
  962.8 3.1 fusion.21
  974.1 3.0 fusion.18
  1002.4 253.6 %all-reduce.6 = (f32[512,8]{1,0:T(8,128)}, f32[512,8]{1,0:T(8,128)}, f32[512,8]{1,0:T(8,128)}) all-reduce(f32[512,8]{1,0:T(8,128)} %reshape.963, f32[512,8]{1,0:T(8,128)} %reshape.953, f32[512,8]{1,0:T(8,128)} %reshape.943), channel_id=10, replica_groups=mesh['kv'=4,'blk'=64] {'blk'}, use_global_device_ids=true, to_apply=%region_33.34.clone | all-reduce | flops 12288 | bytes 98304
  1259.6 13.4 all-to-all-start
  1282.6 19.1 %all-to-all-done = bf16[64,8,1024]{2,1,0:T(8,128)(2,1)} async-done(((bf16[64,8,1024]{2,1,0:T(8,128)(2,1)}), bf16[64,8,1024]{2,1,0:T(8,128)(2,1)}, u32[]{:S(2)}, u32[]{:S(2)}) %all-to-all-start) | async-done | bytes 1048608 | tf_op jit(solution)/shard_map/all_to_all | solution.py:177
  1302.8 5.7 all-to-all-start.1
  1311.5 107.5 %reduce-scatter.8.cloned.1.call-done = f32[8,8,128]{2,1,0:T(8,128)} async-done(((f32[512,8,128]{2,1,0:T(8,128)}), f32[8,8,128]{2,1,0:T(8,128)}) %reduce-scatter.8.cloned.1.call-update) | async-done | bytes 32784 | tf_op jit(solution)/shard_map/reduce_scatter | solution.py:168
  1421.0 8.4 all-to-all-start.2
  1432.9 25.3 %all-to-all-done.2 = bf16[64,8,1024]{2,1,0:T(8,128)(2,1)S(1)} async-done(((bf16[64,8,1024]{2,1,0:T(8,128)(2,1)}), bf16[64,8,1024]{2,1,0:T(8,128)(2,1)S(1)}, u32[]{:S(2)}, u32[]{:S(2)}) %all-to-all-start.2) | async-done | bytes 1048608 | tf_op jit(solution)/shard_map/all_to_all | solution.py:177
  1460.0 43.4 %all-reduce.16.cloned.1.call-done = (f32[512,64]{0,1:T(8,128)}, f32[512,64]{0,1:T(8,128)}, f32[512,64]{0,1:T(8,128)}) async-done(((f32[512,64]{0,1:T(8,128)}, f32[512,64]{0,1:T(8,128)}, f32[512,64]{0,1:T(8,128)}), (f32[512,64]{0,1:T(8,128)}, f32[512,64]{0,1:T(8,128)}, f32[512,64]{0,1:T(8,128)})) %all-reduce.16.cloned.1.call-update) | async-done | bytes 393232 | tf_op jit(solution)/shard_map/psum | solution.py:180
  (267 shorter events, 140.3 us)
Async XLA Ops:
  7.2 1422.3 %copy-start = (bf16[1024,64]{0,1:T(8,128)(2,1)S(1)}, bf16[1024,64]{0,1:T(8,128)(2,1)}, u32[]{:S(2)}) copy-start(bf16[1024,64]{0,1:T(8,128)(2,1)} %param.27) | copy-start | bytes 393220
  7.2 135.0 %copy-start.3 = (bf16[3,512,64]{1,2,0:T(8,128)(2,1)S(1)}, bf16[3,512,64]{1,2,0:T(8,128)(2,1)}, u32[]{:S(2)}) copy-start(bf16[3,512,64]{1,2,0:T(8,128)(2,1)} %param.22) | copy-start | bytes 589828
  7.2 135.0 %copy-start.26 = (f32[64]{0:T(128)S(1)}, f32[64]{0:T(128)}, u32[]{:S(2)}) copy-start(f32[64]{0:T(128)} %param.23) | copy-start | bytes 772
  7.2 343.0 %all-reduce.14.cloned.1.call-start = ((), (), s32[]{:S(2)}) async-start(), calls=%async_computation.12 | async-start | bytes 15728640
  146.4 465.8 %all-gather.6.cloned.1.call-start = ((), (), s32[]{:S(2)}) async-start(), calls=%async_computation.8 | async-start | bytes 1064960 | tf_op jit(solution)/shard_map/all_gather | solution.py:108
  154.3 454.5 %copy-start.24 = (s32[1024]{0:T(1024)}, s32[1024]{0:T(1024)S(1)}, u32[]{:S(2)}) copy-start(s32[1024]{0:T(1024)S(1)} %get-tuple-element.185) | copy-start | bytes 12292
  161.3 7.4 copy-start.27
  352.7 266.1 %all-gather.4.cloned.1.call-start = ((), (), s32[]{:S(2)}) async-start(), calls=%async_computation.6 | async-start | bytes 1064960 | tf_op jit(solution)/shard_map/all_gather | solution.py:108
  473.2 129.1 %copy-start.13 = (pred[32]{0:T(512)(128)(4,1)}, pred[32]{0:T(512)(128)(4,1)S(1)}, u32[]{:S(2)}) copy-start(pred[32]{0:T(512)(128)(4,1)S(1)} %get-tuple-element.121) | copy-start | bytes 100
  473.2 129.1 %copy-start.17 = (s32[32]{0:T(128)}, s32[32]{0:T(128)S(1)}, u32[]{:S(2)}) copy-start(s32[32]{0:T(128)S(1)} %get-tuple-element.124) | copy-start | bytes 388
  474.8 204.5 %all-gather.8.cloned.1.call-start = ((), (), s32[]{:S(2)}) async-start(), calls=%async_computation.10 | async-start | bytes 1064960 | tf_op jit(solution)/shard_map/all_gather | solution.py:108
  482.0 133.2 %copy-start.2 = (bf16[32,1,2,128,128]{4,3,2,1,0:T(8,128)(2,1)S(1)}, bf16[32,1,2,128,128]{4,3,2,1,0:T(8,128)(2,1)}, u32[]{:S(2)}) copy-start(bf16[32,1,2,128,128]{4,3,2,1,0:T(8,128)(2,1)} %param.28) | copy-start | bytes 6291460
  602.3 9.9 copy-start.25
  604.7 652.9 %reduce-scatter.4.cloned.1.call-start = ((), (), s32[]{:S(2)}) async-start(), calls=%async_computation.7 | async-start | bytes 2129920 | tf_op jit(solution)/shard_map/reduce_scatter | solution.py:168
  604.8 76.0 %copy-start.21 = (s32[1024]{0:T(1024)}, s32[1024]{0:T(1024)S(1)}, u32[]{:S(2)}) copy-start(s32[1024]{0:T(1024)S(1)} %pad_clamp_fusion.7) | copy-start | bytes 12292
  968.6 313.1 %reduce-scatter.6.cloned.1.call-start = ((), (), s32[]{:S(2)}) async-start(), calls=%async_computation.9 | async-start | bytes 2129920 | tf_op jit(solution)/shard_map/reduce_scatter | solution.py:168
  999.9 256.8 %copy-start.9 = (f32[8,1,8]{0,2,1:T(8,128)S(1)}, f32[8,1,8]{0,2,1:T(8,128)}, u32[]{:S(2)}) copy-start(f32[8,1,8]{0,2,1:T(8,128)} %copy.332) | copy-start | bytes 772
  1259.6 42.1 %all-to-all-start = ((bf16[64,8,1024]{2,1,0:T(8,128)(2,1)}), bf16[64,8,1024]{2,1,0:T(8,128)(2,1)}, u32[]{:S(2)}, u32[]{:S(2)}) async-start(bf16[64,8,1024]{2,1,0:T(8,128)(2,1)} %stack.30), calls=%async_computation.1 | async-start | bytes 2097152 | tf_op jit(solution)/shard_map/all_to_all | solution.py:177
  1273.0 145.9 %reduce-scatter.8.cloned.1.call-start = ((), (), s32[]{:S(2)}) async-start(), calls=%async_computation.11 | async-start | bytes 2129920 | tf_op jit(solution)/shard_map/reduce_scatter | solution.py:168
  1277.9 32.9 %copy-start.6 = (f32[8,8,3]{1,2,0:T(4,128)S(1)}, f32[8,8,3]{1,2,0:T(4,128)}, u32[]{:S(2)}) copy-start(f32[8,8,3]{1,2,0:T(4,128)} %get-tuple-element.178) | copy-start | bytes 2308
  1302.8 117.1 %all-to-all-start.1 = ((bf16[64,8,1024]{2,1,0:T(8,128)(2,1)}), bf16[64,8,1024]{2,1,0:T(8,128)(2,1)S(1)}, u32[]{:S(2)}, u32[]{:S(2)}) async-start(bf16[64,8,1024]{2,1,0:T(8,128)(2,1)} %stack.32), calls=%async_computation.3 | async-start | bytes 2097152 | tf_op jit(solution)/shard_map/all_to_all | solution.py:177
  1421.0 37.2 %all-to-all-start.2 = ((bf16[64,8,1024]{2,1,0:T(8,128)(2,1)}), bf16[64,8,1024]{2,1,0:T(8,128)(2,1)S(1)}, u32[]{:S(2)}, u32[]{:S(2)}) async-start(bf16[64,8,1024]{2,1,0:T(8,128)(2,1)} %stack.34), calls=%async_computation.5 | async-start | bytes 2097152 | tf_op jit(solution)/shard_map/all_to_all | solution.py:177
  1429.4 29.9 %copy-start.8 = (bf16[3,8,128]{2,0,1:T(4,128)(2,1)S(1)}, bf16[3,8,128]{2,0,1:T(4,128)(2,1)}, u32[]{:S(2)}) copy-start(bf16[3,8,128]{2,0,1:T(4,128)(2,1)} %copy-done.7) | copy-start | bytes 18436
  1429.5 74.0 %all-reduce.16.cloned.1.call-start = ((), (), s32[]{:S(2)}) async-start(), calls=%async_computation.13 | async-start | bytes 786432 | tf_op jit(solution)/shard_map/psum | solution.py:180
  (15 other events, 45.9 us)
Sparse Core Ops, SparseCore 0:
  146.5 203.5 all-reduce.13
  352.9 74.3 all-gather.5
  474.9 74.3 all-gather.3
  604.9 74.3 all-gather.7
  968.7 143.5 reduce-scatter.3
  1116.8 138.9 reduce-scatter.5
  1278.0 140.8 reduce-scatter.7
  1459.5 43.8 all-reduce.15
